TPU v7x, 32 devices: a whole 2x2x4 slice. The times are simulated.
32 devices in a mesh: groups: 2 (over x), fsdp: 8 (over z, y), dp: 2 (over core).
Axes of the slice: x: 2, y: 2, z: 4, core: 2. Of those that a mesh axis runs over, the one named last changes fastest.
Arguments:
- resid: bfloat16 [512, 5120], P(('groups', 'dp'), 'fsdp'), parts along dimension 0, may hold values from -6 to 6
- hidden_act: bfloat16 [512, 6912], P(('groups', 'dp')), parts along dimension 0, may hold values from -11 to 11
- w_down: bfloat16 [6912, 5120], P(None, 'fsdp'), may hold values from -0.078125 to 0.078125
- norm_gain: bfloat16 [5120], P('fsdp'), may hold values from 0.3 to 4, as said below
- head: bfloat16 [5120, 16384], P(None, 'fsdp'), may hold values from -0.25 to 0.25
- data_ids: int32 [512], P(('groups', 'dp')), parts along dimension 0, may hold values from 0 to 16383
- pseudo_ids: int32 [512], P(('groups', 'dp')), parts along dimension 0, may hold values from 0 to 16383
Outputs:
- scores: float32 [512], P(('groups', 'dp')), parts along dimension 0
There are 2 independent parts, one for each index of `groups`. A program takes and returns all parts, laid end to end along the dimension named above; an argument that names none is the same for every part. Nothing has to cross between parts.
Inputs may be any that keep to these rules, and one draw needn't show every extreme that they name: `norm_gain`: positive gains.
All inputs are finite; a program needn't handle non-finite values.
Results may differ from a plain program's by a relative error of at most 0.012.
Values may be sent and summed in bfloat16 or wider, within the bound.
No kernel may reach another device: no remote copies, remote signals or barrier semaphores. Data moves between devices by JAX's collectives and lax.ppermute only.
A program may use at most 192 MiB of HBM per device.

v0:
```python
import jax
import jax.numpy as jnp
from jax import lax
from jax.sharding import PartitionSpec as P

ITERS = 3
cap_value = 30.0
norm_eps = 1e-05
damping = 0.05


def row_total(values):
    return lax.psum(values, "fsdp")


def per_device(resid, hidden_act, w_down, norm_gain, head, data_ids, pseudo_ids):
    tok_rows = hidden_act.shape[0]
    total_rows = tok_rows * lax.axis_size("dp")
    shard_cols = w_down.shape[1]
    width = shard_cols * lax.axis_size("fsdp")
    vocab_cols = head.shape[1]
    vocab_ids = lax.axis_index("fsdp") * vocab_cols + lax.broadcasted_iota(
        jnp.int32, (1, vocab_cols), 1
    )
    gain = norm_gain.astype(jnp.float32)

    def head_logits(normed_shard):
        return jnp.dot(
            lax.all_gather(normed_shard, "fsdp", axis=1, tiled=True),
            head,
            preferred_element_type=jnp.float32,
        )

    def head_project(weighted):
        return (
            lax.psum_scatter(
                lax.dot_general(
                    head, weighted, (((1,), (1,)), ((), ())), preferred_element_type=jnp.float32
                ).astype(jnp.bfloat16),
                "fsdp",
                scatter_dimension=0,
                tiled=True,
            )
            .astype(jnp.float32)
            .T
        )

    z = resid.astype(jnp.float32) + jnp.dot(hidden_act, w_down, preferred_element_type=jnp.float32)
    inv = lax.rsqrt(row_total(jnp.sum(z * z, axis=1, keepdims=True)) / width + norm_eps)
    normed = (z * inv * gain).astype(jnp.bfloat16)
    capped = cap_value * jnp.tanh(head_logits(normed) / cap_value)
    slope = 1.0 - (capped / cap_value) ** 2
    expval = jnp.exp(capped)
    prob = expval / row_total(jnp.sum(expval, axis=1, keepdims=True))

    def norm_back(upstream):
        scaled = gain * head_project((upstream * slope).astype(jnp.bfloat16))
        mixed = row_total(jnp.sum(z * scaled, axis=1, keepdims=True)) / width
        return inv * scaled - z * inv**3 * mixed

    def tangent(full_vector):
        zv = jnp.dot(hidden_act, full_vector, preferred_element_type=jnp.float32)
        inv_t = -(inv**3) * row_total(jnp.sum(z * zv, axis=1, keepdims=True)) / width
        moved = (gain * (zv * inv + z * inv_t)).astype(jnp.bfloat16)
        return slope * head_logits(moved)

    def full_rows(vector):
        return lax.all_gather(vector.astype(jnp.bfloat16), "dp", axis=0, tiled=True)

    def param_sum(dz):
        local = lax.dot_general(
            hidden_act,
            dz.astype(jnp.bfloat16),
            (((0,), (0,)), ((), ())),
            preferred_element_type=jnp.float32,
        )
        return lax.psum_scatter(
            local.astype(jnp.bfloat16), "dp", scatter_dimension=0, tiled=True
        ).astype(jnp.float32)

    def global_dot(values):
        return lax.psum(values, ("fsdp", "dp"))

    pseudo_hot = (pseudo_ids[:, None] == vocab_ids).astype(jnp.float32)
    grad = param_sum(norm_back((prob - pseudo_hot) / total_rows))
    solution = jnp.zeros_like(grad)
    remain = grad
    search = grad
    norm_now = global_dot(jnp.sum(remain * remain))
    for step in range(ITERS):
        change = tangent(full_rows(search))
        inner = row_total(jnp.sum(prob * change, axis=1, keepdims=True))
        image = param_sum(norm_back((prob * change - prob * inner) / total_rows)) + damping * search
        alpha = norm_now / global_dot(jnp.sum(search * image))
        solution = solution + alpha * search
        remain = remain - alpha * image
        if step + 1 < ITERS:
            norm_next = global_dot(jnp.sum(remain * remain))
            search = remain + norm_next / norm_now * search
            norm_now = norm_next
    data_hot = (data_ids[:, None] == vocab_ids).astype(jnp.float32)
    return row_total(jnp.sum((prob - data_hot) * tangent(full_rows(solution)), axis=1))


def solution(mesh):
    placed = (
        P(("groups", "dp"), "fsdp"),
        P(("groups", "dp"), None),
        P(None, "fsdp"),
        P("fsdp"),
        P(None, "fsdp"),
        P(("groups", "dp")),
        P(("groups", "dp")),
    )
    return jax.shard_map(
        per_device, mesh=mesh, in_specs=placed, out_specs=P(("groups", "dp")), check_vma=False
    )
```

profile of v0, /device:TPU:0, one launch (start us, length us, event | category | flops | bytes accessed | tf_op | source)
XLA Modules:
  0.0 1366.7 jit_solution(14872717110527854634)
XLA Ops:
  13.2 23.2 %psum.140 = f32[128,1]{0,1:T(1,128)S(1)} all-reduce(f32[128,1]{0,1:T(1,128)S(1)} %bitcast.129), channel_id=1, replica_groups=mesh['groups'=2,'fsdp'=8,'dp'=2] {'fsdp'}, use_global_device_ids=true, to_apply=%region_1.0 | all-reduce | flops 128 | bytes 1024 | tf_op jit(solution)/shard_map/psum | solution.py:13
  37.2 39.9 %all-gather.10.cloned.1.call-done = bf16[128,5120]{1,0:T(8,128)(2,1)} async-done(((bf16[128,640]{1,0:T(8,128)(2,1)}), bf16[128,5120]{1,0:T(8,128)(2,1)}) %all-gather.10.cloned.1.call-update) | async-done | bytes 1310736 | tf_op jit(solution)/shard_map/all_gather | solution.py:29
  88.4 19.0 %psum.141 = f32[128]{0:T(128)S(1)} all-reduce(f32[128]{0:T(128)S(1)} %get-tuple-element.17), channel_id=1, replica_groups=mesh['groups'=2,'fsdp'=8,'dp'=2] {'fsdp'}, use_global_device_ids=true, to_apply=%region_3.0 | all-reduce | flops 128 | bytes 1024 | tf_op jit(solution)/shard_map/psum | solution.py:13
  120.5 62.6 %reduce-scatter.25.cloned.1.call-done = bf16[640,128]{1,0:T(8,128)(2,1)} async-done(((bf16[5120,128]{1,0:T(8,128)(2,1)}), bf16[640,128]{1,0:T(8,128)(2,1)}) %reduce-scatter.25.cloned.1.call-update) | async-done | bytes 163856
  184.2 19.0 %psum.142 = f32[128,1]{0,1:T(1,128)S(1)} all-reduce(f32[128,1]{0,1:T(1,128)S(1)} %bitcast.130), channel_id=1, replica_groups=mesh['groups'=2,'fsdp'=8,'dp'=2] {'fsdp'}, use_global_device_ids=true, to_apply=%region_6.0 | all-reduce | flops 128 | bytes 1024 | tf_op jit(solution)/shard_map/psum | solution.py:13
  243.5 22.2 %all-gather.12.cloned.1.call-done = bf16[6912,640]{0,1:T(8,128)(2,1)} async-done(((bf16[3456,640]{0,1:T(8,128)(2,1)}), bf16[6912,640]{0,1:T(8,128)(2,1)}) %all-gather.12.cloned.1.call-update) | async-done | bytes 8847376 | tf_op jit(solution)/shard_map/all_gather | solution.py:68
  272.1 21.6 %psum.144 = f32[128,1]{0,1:T(1,128)S(1)} all-reduce(f32[128,1]{0,1:T(1,128)S(1)} %bitcast.134), channel_id=1, replica_groups=mesh['groups'=2,'fsdp'=8,'dp'=2] {'fsdp'}, use_global_device_ids=true, to_apply=%region_11.0 | all-reduce | flops 128 | bytes 1024 | tf_op jit(solution)/shard_map/psum | solution.py:13
  294.6 39.9 %all-gather.14.cloned.1.call-done = bf16[128,5120]{1,0:T(8,128)(2,1)} async-done(((bf16[128,640]{1,0:T(8,128)(2,1)}), bf16[128,5120]{1,0:T(8,128)(2,1)}) %all-gather.14.cloned.1.call-update) | async-done | bytes 1310736 | tf_op jit(solution)/shard_map/all_gather | solution.py:29
  346.0 19.0 %psum.145 = f32[128]{0:T(128)S(1)} all-reduce(f32[128]{0:T(128)S(1)} %get-tuple-element.21), channel_id=1, replica_groups=mesh['groups'=2,'fsdp'=8,'dp'=2] {'fsdp'}, use_global_device_ids=true, to_apply=%region_13.0 | all-reduce | flops 128 | bytes 1024 | tf_op jit(solution)/shard_map/psum | solution.py:13
  378.4 62.5 %reduce-scatter.29.cloned.1.call-done = bf16[640,128]{1,0:T(8,128)(2,1)} async-done(((bf16[5120,128]{1,0:T(8,128)(2,1)}), bf16[640,128]{1,0:T(8,128)(2,1)}) %reduce-scatter.29.cloned.1.call-update) | async-done | bytes 163856
  442.1 19.2 %psum.146 = f32[128,1]{0,1:T(1,128)S(1)} all-reduce(f32[128,1]{0,1:T(1,128)S(1)} %bitcast.131), channel_id=1, replica_groups=mesh['groups'=2,'fsdp'=8,'dp'=2] {'fsdp'}, use_global_device_ids=true, to_apply=%region_16.0 | all-reduce | flops 128 | bytes 1024 | tf_op jit(solution)/shard_map/psum | solution.py:13
  506.5 34.5 %all-reduce = (f32[]{:T(128)}, f32[]{:T(128)}) all-reduce(f32[]{:T(128)} %get-tuple-element.6, f32[]{:T(128)} %get-tuple-element.5), channel_id=1, replica_groups=mesh['groups'=2,'fsdp'=8,'dp'=2] {'fsdp','dp'}, use_global_device_ids=true, to_apply=%region_9.0 | all-reduce | flops 2 | bytes 16 | tf_op jit(solution)/shard_map/psum | solution.py:82
  548.7 30.1 %psum.148 = f32[]{:T(128)} all-reduce(f32[]{:T(128)} %multiply_reduce_fusion.3), channel_id=1, replica_groups=mesh['groups'=2,'fsdp'=8,'dp'=2] {'fsdp','dp'}, use_global_device_ids=true, to_apply=%region_21.0 | all-reduce | flops 1 | bytes 8 | tf_op jit(solution)/shard_map/psum | solution.py:82
  588.4 18.3 %all-gather.16.cloned.1.call-done = bf16[6912,640]{0,1:T(8,128)(2,1)} async-done(((bf16[3456,640]{0,1:T(8,128)(2,1)}), bf16[6912,640]{0,1:T(8,128)(2,1)}) %all-gather.16.cloned.1.call-update) | async-done | bytes 8847376 | tf_op jit(solution)/shard_map/all_gather | solution.py:68
  613.1 21.6 %psum.149 = f32[128,1]{0,1:T(1,128)S(1)} all-reduce(f32[128,1]{0,1:T(1,128)S(1)} %bitcast.135), channel_id=1, replica_groups=mesh['groups'=2,'fsdp'=8,'dp'=2] {'fsdp'}, use_global_device_ids=true, to_apply=%region_23.0 | all-reduce | flops 128 | bytes 1024 | tf_op jit(solution)/shard_map/psum | solution.py:13
  635.6 39.9 %all-gather.18.cloned.1.call-done = bf16[128,5120]{1,0:T(8,128)(2,1)} async-done(((bf16[128,640]{1,0:T(8,128)(2,1)}), bf16[128,5120]{1,0:T(8,128)(2,1)}) %all-gather.18.cloned.1.call-update) | async-done | bytes 1310736 | tf_op jit(solution)/shard_map/all_gather | solution.py:29
  687.0 19.1 %psum.150 = f32[128]{0:T(128)S(1)} all-reduce(f32[128]{0:T(128)S(1)} %get-tuple-element.25), channel_id=1, replica_groups=mesh['groups'=2,'fsdp'=8,'dp'=2] {'fsdp'}, use_global_device_ids=true, to_apply=%region_25.0 | all-reduce | flops 128 | bytes 1024 | tf_op jit(solution)/shard_map/psum | solution.py:13
  719.5 62.5 %reduce-scatter.33.cloned.1.call-done = bf16[640,128]{1,0:T(8,128)(2,1)} async-done(((bf16[5120,128]{1,0:T(8,128)(2,1)}), bf16[640,128]{1,0:T(8,128)(2,1)}) %reduce-scatter.33.cloned.1.call-update) | async-done | bytes 163856
  783.3 19.1 %psum.151 = f32[128,1]{0,1:T(1,128)S(1)} all-reduce(f32[128,1]{0,1:T(1,128)S(1)} %bitcast.132), channel_id=1, replica_groups=mesh['groups'=2,'fsdp'=8,'dp'=2] {'fsdp'}, use_global_device_ids=true, to_apply=%region_28.0 | all-reduce | flops 128 | bytes 1024 | tf_op jit(solution)/shard_map/psum | solution.py:13
  849.7 34.5 %psum.152 = f32[]{:T(128)} all-reduce(f32[]{:T(128)} %multiply_reduce_fusion.2), channel_id=1, replica_groups=mesh['groups'=2,'fsdp'=8,'dp'=2] {'fsdp','dp'}, use_global_device_ids=true, to_apply=%region_31.0 | all-reduce | flops 1 | bytes 8 | tf_op jit(solution)/shard_map/psum | solution.py:82
  893.3 30.3 %psum.153 = f32[]{:T(128)} all-reduce(f32[]{:T(128)} %multiply_reduce_fusion.1), channel_id=1, replica_groups=mesh['groups'=2,'fsdp'=8,'dp'=2] {'fsdp','dp'}, use_global_device_ids=true, to_apply=%region_33.0 | all-reduce | flops 1 | bytes 8 | tf_op jit(solution)/shard_map/psum | solution.py:82
  935.1 18.4 %all-gather.20.cloned.1.call-done = bf16[6912,640]{0,1:T(8,128)(2,1)} async-done(((bf16[3456,640]{0,1:T(8,128)(2,1)}), bf16[6912,640]{0,1:T(8,128)(2,1)}) %all-gather.20.cloned.1.call-update) | async-done | bytes 8847376 | tf_op jit(solution)/shard_map/all_gather | solution.py:68
  959.9 21.6 %psum.154 = f32[128,1]{0,1:T(1,128)S(1)} all-reduce(f32[128,1]{0,1:T(1,128)S(1)} %bitcast.136), channel_id=1, replica_groups=mesh['groups'=2,'fsdp'=8,'dp'=2] {'fsdp'}, use_global_device_ids=true, to_apply=%region_35.0 | all-reduce | flops 128 | bytes 1024 | tf_op jit(solution)/shard_map/psum | solution.py:13
  982.4 39.9 %all-gather.22.cloned.1.call-done = bf16[128,5120]{1,0:T(8,128)(2,1)} async-done(((bf16[128,640]{1,0:T(8,128)(2,1)}), bf16[128,5120]{1,0:T(8,128)(2,1)}) %all-gather.22.cloned.1.call-update) | async-done | bytes 1310736 | tf_op jit(solution)/shard_map/all_gather | solution.py:29
  1033.8 19.0 %psum.155 = f32[128]{0:T(128)S(1)} all-reduce(f32[128]{0:T(128)S(1)} %get-tuple-element.29), channel_id=1, replica_groups=mesh['groups'=2,'fsdp'=8,'dp'=2] {'fsdp'}, use_global_device_ids=true, to_apply=%region_37.0 | all-reduce | flops 128 | bytes 1024 | tf_op jit(solution)/shard_map/psum | solution.py:13
  1066.1 62.5 %reduce-scatter.37.cloned.1.call-done = bf16[640,128]{1,0:T(8,128)(2,1)} async-done(((bf16[5120,128]{1,0:T(8,128)(2,1)}), bf16[640,128]{1,0:T(8,128)(2,1)}) %reduce-scatter.37.cloned.1.call-update) | async-done | bytes 163856
  1129.7 19.5 %psum.156 = f32[128,1]{0,1:T(1,128)S(1)} all-reduce(f32[128,1]{0,1:T(1,128)S(1)} %bitcast.133), channel_id=1, replica_groups=mesh['groups'=2,'fsdp'=8,'dp'=2] {'fsdp'}, use_global_device_ids=true, to_apply=%region_40.0 | all-reduce | flops 128 | bytes 1024 | tf_op jit(solution)/shard_map/psum | solution.py:13
  1196.7 34.5 %psum.157 = f32[]{:T(128)} all-reduce(f32[]{:T(128)} %multiply_reduce_fusion), channel_id=1, replica_groups=mesh['groups'=2,'fsdp'=8,'dp'=2] {'fsdp','dp'}, use_global_device_ids=true, to_apply=%region_43.0 | all-reduce | flops 1 | bytes 8 | tf_op jit(solution)/shard_map/psum | solution.py:82
  1242.1 18.3 %all-gather.24.cloned.1.call-done = bf16[6912,640]{0,1:T(8,128)(2,1)} async-done(((bf16[3456,640]{0,1:T(8,128)(2,1)}), bf16[6912,640]{0,1:T(8,128)(2,1)}) %all-gather.24.cloned.1.call-update) | async-done | bytes 8847376 | tf_op jit(solution)/shard_map/all_gather | solution.py:68
  1266.8 21.9 %psum.158 = f32[128,1]{0,1:T(1,128)S(1)} all-reduce(f32[128,1]{0,1:T(1,128)S(1)} %bitcast.137), channel_id=1, replica_groups=mesh['groups'=2,'fsdp'=8,'dp'=2] {'fsdp'}, use_global_device_ids=true, to_apply=%region_45.0 | all-reduce | flops 128 | bytes 1024 | tf_op jit(solution)/shard_map/psum | solution.py:13
  1289.5 39.9 %all-gather.26.cloned.1.call-done = bf16[128,5120]{1,0:T(8,128)(2,1)} async-done(((bf16[128,640]{1,0:T(8,128)(2,1)}), bf16[128,5120]{1,0:T(8,128)(2,1)}) %all-gather.26.cloned.1.call-update) | async-done | bytes 1310736 | tf_op jit(solution)/shard_map/all_gather | solution.py:29
  1340.2 19.5 %psum.159 = f32[128]{0:T(128)} all-reduce(f32[128]{0:T(128)S(1)} %fusion.21), channel_id=1, replica_groups=mesh['groups'=2,'fsdp'=8,'dp'=2] {'fsdp'}, use_global_device_ids=true, to_apply=%region_47.0 | all-reduce | flops 128 | bytes 1024 | tf_op jit(solution)/shard_map/psum | solution.py:13
  (118 shorter events, 373.7 us)
Async XLA Ops:
  6.5 1.5 copy-start
  6.5 70.6 %all-gather.10.cloned.1.call-start = ((), (), s32[]{:S(2)}) async-start(), calls=%async_computation.8 | async-start | bytes 1474560 | tf_op jit(solution)/shard_map/all_gather | solution.py:29
  37.1 145.9 %reduce-scatter.25.cloned.1.call-start = ((), (), s32[]{:S(2)}) async-start(), calls=%async_computation.17 | async-start | bytes 1474560
  37.2 70.2 %copy-start.5 = (s32[2048]{0:T(1024)}, s32[2048]{0:T(1024)S(1)}, u32[]{:S(2)}) copy-start(s32[2048]{0:T(1024)S(1)} %iota_add_fusion) | copy-start | bytes 24580
  37.2 70.2 %copy-start.7 = (s32[128]{0:T(128)S(1)}, s32[128]{0:T(128)}, u32[]{:S(2)}) copy-start(s32[128]{0:T(128)} %param.13) | copy-start | bytes 1540
  120.4 115.6 %reduce-scatter.27.cloned.1.call-start = ((), (), s32[]{:S(2)}) async-start(), calls=%async_computation.18 | async-start | bytes 13271040
  221.9 43.8 %all-gather.12.cloned.1.call-start = ((), (), s32[]{:S(2)}) async-start(), calls=%async_computation.9 | async-start | bytes 13271040 | tf_op jit(solution)/shard_map/all_gather | solution.py:68
  243.2 91.2 %copy-start.1 = (f32[128,2048]{1,0:T(8,128)S(1)}, f32[128,2048]{1,0:T(8,128)}, u32[]{:S(2)}) copy-start(f32[128,2048]{1,0:T(8,128)} %get-tuple-element.18) | copy-start | bytes 3145732
  243.3 91.2 %all-gather.14.cloned.1.call-start = ((), (), s32[]{:S(2)}) async-start(), calls=%async_computation.10 | async-start | bytes 1474560 | tf_op jit(solution)/shard_map/all_gather | solution.py:29
  294.5 146.3 %reduce-scatter.29.cloned.1.call-start = ((), (), s32[]{:S(2)}) async-start(), calls=%async_computation.19 | async-start | bytes 1474560
  378.4 115.5 %reduce-scatter.31.cloned.1.call-start = ((), (), s32[]{:S(2)}) async-start(), calls=%async_computation.20 | async-start | bytes 13271040
  479.9 126.8 %all-gather.16.cloned.1.call-start = ((), (), s32[]{:S(2)}) async-start(), calls=%async_computation.11 | async-start | bytes 13271040 | tf_op jit(solution)/shard_map/all_gather | solution.py:68
  588.3 87.2 %copy-start.2 = (f32[128,2048]{1,0:T(8,128)S(1)}, f32[128,2048]{1,0:T(8,128)}, u32[]{:S(2)}) copy-start(f32[128,2048]{1,0:T(8,128)} %get-tuple-element.18) | copy-start | bytes 3145732
  588.3 87.2 %all-gather.18.cloned.1.call-start = ((), (), s32[]{:S(2)}) async-start(), calls=%async_computation.12 | async-start | bytes 1474560 | tf_op jit(solution)/shard_map/all_gather | solution.py:29
  635.5 146.6 %reduce-scatter.33.cloned.1.call-start = ((), (), s32[]{:S(2)}) async-start(), calls=%async_computation.21 | async-start | bytes 1474560
  719.5 115.6 %reduce-scatter.35.cloned.1.call-start = ((), (), s32[]{:S(2)}) async-start(), calls=%async_computation.22 | async-start | bytes 13271040
  821.0 132.5 %all-gather.20.cloned.1.call-start = ((), (), s32[]{:S(2)}) async-start(), calls=%async_computation.13 | async-start | bytes 13271040 | tf_op jit(solution)/shard_map/all_gather | solution.py:68
  935.1 87.2 %copy-start.3 = (f32[128,2048]{1,0:T(8,128)S(1)}, f32[128,2048]{1,0:T(8,128)}, u32[]{:S(2)}) copy-start(f32[128,2048]{1,0:T(8,128)} %get-tuple-element.18) | copy-start | bytes 3145732
  935.1 87.2 %all-gather.22.cloned.1.call-start = ((), (), s32[]{:S(2)}) async-start(), calls=%async_computation.14 | async-start | bytes 1474560 | tf_op jit(solution)/shard_map/all_gather | solution.py:29
  982.3 146.2 %reduce-scatter.37.cloned.1.call-start = ((), (), s32[]{:S(2)}) async-start(), calls=%async_computation.23 | async-start | bytes 1474560
  1066.0 115.9 %reduce-scatter.39.cloned.1.call-start = ((), (), s32[]{:S(2)}) async-start(), calls=%async_computation.24 | async-start | bytes 13271040
  1167.8 92.6 %all-gather.24.cloned.1.call-start = ((), (), s32[]{:S(2)}) async-start(), calls=%async_computation.15 | async-start | bytes 13271040 | tf_op jit(solution)/shard_map/all_gather | solution.py:68
  1242.0 87.5 %copy-start.4 = (f32[128,2048]{1,0:T(8,128)S(1)}, f32[128,2048]{1,0:T(8,128)}, u32[]{:S(2)}) copy-start(f32[128,2048]{1,0:T(8,128)} %get-tuple-element.18) | copy-start | bytes 3145732
  1242.0 87.5 %copy-start.6 = (s32[2048]{0:T(1024)S(1)}, s32[2048]{0:T(1024)}, u32[]{:S(2)}) copy-start(s32[2048]{0:T(1024)} %copy-done.5) | copy-start | bytes 24580
  1242.0 87.5 %copy-start.8 = (s32[128]{0:T(128)S(1)}, s32[128]{0:T(128)}, u32[]{:S(2)}) copy-start(s32[128]{0:T(128)} %param.12) | copy-start | bytes 1540
  1242.0 87.4 %all-gather.26.cloned.1.call-start = ((), (), s32[]{:S(2)}) async-start(), calls=%async_computation.16 | async-start | bytes 1474560 | tf_op jit(solution)/shard_map/all_gather | solution.py:29
Sparse Core Ops, SparseCore 0:
  37.2 39.7 all-gather.9
  120.5 62.4 reduce-scatter.24
  222.0 13.9 reduce-scatter.26
  243.4 22.2 all-gather.11
  294.6 39.7 all-gather.13
  378.5 62.3 reduce-scatter.28
  480.0 13.8 reduce-scatter.30
  588.4 18.2 all-gather.15
  635.6 39.7 all-gather.17
  719.6 62.4 reduce-scatter.32
  821.1 13.9 reduce-scatter.34
  935.2 18.2 all-gather.19
  982.4 39.7 all-gather.21
  1066.1 62.3 reduce-scatter.36
  1167.9 13.9 reduce-scatter.38
  1242.1 18.2 all-gather.23
  1289.6 39.7 all-gather.25
where the time goes:
time: 1380 us; the launch traced here: 1370 us
  waiting for transfers between devices  583 us (42%)
  blocking collectives  446 us (32%)
  matrix products  159 us (12%)
  local copies, waits for them, and re-layouts  89.8 us (7%)
  other arithmetic  68 us (5%)
  between operations  20.3 us (1%)
    unnamed x25, waiting for transfers between devices  306 us
    psum x14, blocking collectives, row_total(): return lax.psum(values, 'fsdp')  282 us
    all_gather x5, waiting for transfers between devices, head_logits(): lax.all_gather(normed_shard, 'fsdp', axis=1, tiled=True)  199 us
    psum x5, blocking collectives, global_dot(): return lax.psum(values, ('fsdp', 'dp'))  164 us
    unnamed x34, local copies, waits for them, and re-layouts  89.8 us
    all_gather x4, waiting for transfers between devices, full_rows(): return lax.all_gather(vector.astype(jnp.bfloat16), 'dp', axis=0, tiled=True)  77.2 us
    dot_general x5, matrix products, head_logits(): jnp.dot(lax.all_gather(normed_shard, 'fsdp', axis=1, tiled=True), head, p...  56.8 us
    dot_general x4, matrix products, head_project(): lax.dot_general(head, weighted, (((1,), (1,)), ((), ())), preferred_eleme...  47 us
  transfers between devices with their start and end apart: 17, of which 17 were waited for; matrix products, arithmetic and copies ran while one was open for 0% of the time, Pallas kernels for 0%

commit v1 on v0

--- a/solution.py
+++ b/solution.py
@@ -79,7 +79,7 @@
         ).astype(jnp.float32)
 
     def global_dot(values):
-        return lax.psum(values, ("fsdp", "dp"))
+        return jnp.sum(lax.all_gather(values, ("fsdp", "dp")), axis=0)
 
     pseudo_hot = (pseudo_ids[:, None] == vocab_ids).astype(jnp.float32)
     grad = param_sum(norm_back((prob - pseudo_hot) / total_rows))

time: 1380 us -> 1390 us (level)
    psum x5 -> x0, blocking collectives: 164 us -> none  [global_dot(): return lax.psum(values, ('fsdp', 'dp'))]
    unnamed x0 -> x5, blocking collectives: none -> 161 us
    unnamed x34 -> x49, local copies, waits for them, and re-layouts: 89.8 us -> 98.8 us
where the time goes in v1:
time: 1390 us; the launch traced here: 1370 us
  waiting for transfers between devices  581 us (42%)
  blocking collectives  442 us (32%)
  matrix products  159 us (11%)
  local copies, waits for them, and re-layouts  98.8 us (7%)
  other arithmetic  71.9 us (5%)
  between operations  20.3 us (1%)
    unnamed x25, waiting for transfers between devices  305 us
    psum x14, blocking collectives, row_total(): return lax.psum(values, 'fsdp')  282 us
    all_gather x5, waiting for transfers between devices, head_logits(): lax.all_gather(normed_shard, 'fsdp', axis=1, tiled=True)  199 us
    unnamed x5, blocking collectives  161 us
    unnamed x49, local copies, waits for them, and re-layouts  98.8 us
    all_gather x4, waiting for transfers between devices, full_rows(): return lax.all_gather(vector.astype(jnp.bfloat16), 'dp', axis=0, tiled=True)  76.8 us
    dot_general x5, matrix products, head_logits(): jnp.dot(lax.all_gather(normed_shard, 'fsdp', axis=1, tiled=True), head, p...  56.8 us
    dot_general x4, matrix products, head_project(): lax.dot_general(head, weighted, (((1,), (1,)), ((), ())), preferred_eleme...  47 us
  transfers between devices with their start and end apart: 17, of which 17 were waited for; matrix products, arithmetic and copies ran while one was open for 0% of the time, Pallas kernels for 0%

profile of v1, /device:TPU:0, one launch (start us, length us, event | category | flops | bytes accessed | tf_op | source)
XLA Modules:
  0.0 1374.9 jit_solution(4984758867359583961)
XLA Ops:
  13.2 23.2 %psum.98 = f32[128,1]{0,1:T(1,128)S(1)} all-reduce(f32[128,1]{0,1:T(1,128)S(1)} %bitcast.136), channel_id=1, replica_groups=mesh['groups'=2,'fsdp'=8,'dp'=2] {'fsdp'}, use_global_device_ids=true, to_apply=%region_1.0 | all-reduce | flops 128 | bytes 1024 | tf_op jit(solution)/shard_map/psum | solution.py:13
  37.2 39.9 %all-gather.10.cloned.1.call-done = bf16[128,5120]{1,0:T(8,128)(2,1)} async-done(((bf16[128,640]{1,0:T(8,128)(2,1)}), bf16[128,5120]{1,0:T(8,128)(2,1)}) %all-gather.10.cloned.1.call-update) | async-done | bytes 1310736 | tf_op jit(solution)/shard_map/all_gather | solution.py:29
  88.4 19.0 %psum.99 = f32[128]{0:T(128)S(1)} all-reduce(f32[128]{0:T(128)S(1)} %get-tuple-element.17), channel_id=1, replica_groups=mesh['groups'=2,'fsdp'=8,'dp'=2] {'fsdp'}, use_global_device_ids=true, to_apply=%region_3.0 | all-reduce | flops 128 | bytes 1024 | tf_op jit(solution)/shard_map/psum | solution.py:13
  120.4 62.4 %reduce-scatter.25.cloned.1.call-done = bf16[640,128]{1,0:T(8,128)(2,1)} async-done(((bf16[5120,128]{1,0:T(8,128)(2,1)}), bf16[640,128]{1,0:T(8,128)(2,1)}) %reduce-scatter.25.cloned.1.call-update) | async-done | bytes 163856
  184.1 19.1 %psum.100 = f32[128,1]{0,1:T(1,128)S(1)} all-reduce(f32[128,1]{0,1:T(1,128)S(1)} %bitcast.137), channel_id=1, replica_groups=mesh['groups'=2,'fsdp'=8,'dp'=2] {'fsdp'}, use_global_device_ids=true, to_apply=%region_6.0 | all-reduce | flops 128 | bytes 1024 | tf_op jit(solution)/shard_map/psum | solution.py:13
  243.6 21.9 %all-gather.12.cloned.1.call-done = bf16[6912,640]{0,1:T(8,128)(2,1)} async-done(((bf16[3456,640]{0,1:T(8,128)(2,1)}), bf16[6912,640]{0,1:T(8,128)(2,1)}) %all-gather.12.cloned.1.call-update) | async-done | bytes 8847376 | tf_op jit(solution)/shard_map/all_gather | solution.py:68
  271.9 21.6 %psum.101 = f32[128,1]{0,1:T(1,128)S(1)} all-reduce(f32[128,1]{0,1:T(1,128)S(1)} %bitcast.141), channel_id=1, replica_groups=mesh['groups'=2,'fsdp'=8,'dp'=2] {'fsdp'}, use_global_device_ids=true, to_apply=%region_11.0 | all-reduce | flops 128 | bytes 1024 | tf_op jit(solution)/shard_map/psum | solution.py:13
  294.5 39.9 %all-gather.14.cloned.1.call-done = bf16[128,5120]{1,0:T(8,128)(2,1)} async-done(((bf16[128,640]{1,0:T(8,128)(2,1)}), bf16[128,5120]{1,0:T(8,128)(2,1)}) %all-gather.14.cloned.1.call-update) | async-done | bytes 1310736 | tf_op jit(solution)/shard_map/all_gather | solution.py:29
  345.9 19.0 %psum.102 = f32[128]{0:T(128)S(1)} all-reduce(f32[128]{0:T(128)S(1)} %get-tuple-element.21), channel_id=1, replica_groups=mesh['groups'=2,'fsdp'=8,'dp'=2] {'fsdp'}, use_global_device_ids=true, to_apply=%region_13.0 | all-reduce | flops 128 | bytes 1024 | tf_op jit(solution)/shard_map/psum | solution.py:13
  378.3 62.5 %reduce-scatter.29.cloned.1.call-done = bf16[640,128]{1,0:T(8,128)(2,1)} async-done(((bf16[5120,128]{1,0:T(8,128)(2,1)}), bf16[640,128]{1,0:T(8,128)(2,1)}) %reduce-scatter.29.cloned.1.call-update) | async-done | bytes 163856
  441.9 19.2 %psum.103 = f32[128,1]{0,1:T(1,128)S(1)} all-reduce(f32[128,1]{0,1:T(1,128)S(1)} %bitcast.138), channel_id=1, replica_groups=mesh['groups'=2,'fsdp'=8,'dp'=2] {'fsdp'}, use_global_device_ids=true, to_apply=%region_16.0 | all-reduce | flops 128 | bytes 1024 | tf_op jit(solution)/shard_map/psum | solution.py:13
  509.1 33.8 %all-reduce.6 = (f32[16]{0:T(128)S(1)}, f32[16]{0:T(128)S(1)}) all-reduce(f32[16]{0:T(128)S(1)} %dynamic-update-slice, f32[16]{0:T(128)S(1)} %dynamic-update-slice.1), channel_id=1, replica_groups=mesh['groups'=2,'fsdp'=8,'dp'=2] {'fsdp','dp'}, use_global_device_ids=true, to_apply=%add | all-reduce | flops 32 | bytes 256
  553.5 29.5 %all-reduce.2 = f32[16]{0:T(128)S(1)} all-reduce(f32[16]{0:T(128)S(1)} %dynamic-update-slice.2), channel_id=1, replica_groups=mesh['groups'=2,'fsdp'=8,'dp'=2] {'fsdp','dp'}, use_global_device_ids=true, to_apply=%add.2 | all-reduce | flops 16 | bytes 128
  593.2 18.3 %all-gather.16.cloned.1.call-done = bf16[6912,640]{0,1:T(8,128)(2,1)} async-done(((bf16[3456,640]{0,1:T(8,128)(2,1)}), bf16[6912,640]{0,1:T(8,128)(2,1)}) %all-gather.16.cloned.1.call-update) | async-done | bytes 8847376 | tf_op jit(solution)/shard_map/all_gather | solution.py:68
  617.9 21.6 %psum.104 = f32[128,1]{0,1:T(1,128)S(1)} all-reduce(f32[128,1]{0,1:T(1,128)S(1)} %bitcast.142), channel_id=1, replica_groups=mesh['groups'=2,'fsdp'=8,'dp'=2] {'fsdp'}, use_global_device_ids=true, to_apply=%region_23.0 | all-reduce | flops 128 | bytes 1024 | tf_op jit(solution)/shard_map/psum | solution.py:13
  640.6 39.7 %all-gather.18.cloned.1.call-done = bf16[128,5120]{1,0:T(8,128)(2,1)} async-done(((bf16[128,640]{1,0:T(8,128)(2,1)}), bf16[128,5120]{1,0:T(8,128)(2,1)}) %all-gather.18.cloned.1.call-update) | async-done | bytes 1310736 | tf_op jit(solution)/shard_map/all_gather | solution.py:29
  691.9 19.0 %psum.105 = f32[128]{0:T(128)S(1)} all-reduce(f32[128]{0:T(128)S(1)} %get-tuple-element.25), channel_id=1, replica_groups=mesh['groups'=2,'fsdp'=8,'dp'=2] {'fsdp'}, use_global_device_ids=true, to_apply=%region_25.0 | all-reduce | flops 128 | bytes 1024 | tf_op jit(solution)/shard_map/psum | solution.py:13
  724.2 62.4 %reduce-scatter.33.cloned.1.call-done = bf16[640,128]{1,0:T(8,128)(2,1)} async-done(((bf16[5120,128]{1,0:T(8,128)(2,1)}), bf16[640,128]{1,0:T(8,128)(2,1)}) %reduce-scatter.33.cloned.1.call-update) | async-done | bytes 163856
  787.8 19.1 %psum.106 = f32[128,1]{0,1:T(1,128)S(1)} all-reduce(f32[128,1]{0,1:T(1,128)S(1)} %bitcast.139), channel_id=1, replica_groups=mesh['groups'=2,'fsdp'=8,'dp'=2] {'fsdp'}, use_global_device_ids=true, to_apply=%region_28.0 | all-reduce | flops 128 | bytes 1024 | tf_op jit(solution)/shard_map/psum | solution.py:13
  855.5 34.2 %all-reduce.3 = f32[16]{0:T(128)S(1)} all-reduce(f32[16]{0:T(128)S(1)} %dynamic-update-slice.3), channel_id=1, replica_groups=mesh['groups'=2,'fsdp'=8,'dp'=2] {'fsdp','dp'}, use_global_device_ids=true, to_apply=%add.3 | all-reduce | flops 16 | bytes 128
  900.9 29.5 %all-reduce.4 = f32[16]{0:T(128)S(1)} all-reduce(f32[16]{0:T(128)S(1)} %dynamic-update-slice.4), channel_id=1, replica_groups=mesh['groups'=2,'fsdp'=8,'dp'=2] {'fsdp','dp'}, use_global_device_ids=true, to_apply=%add.4 | all-reduce | flops 16 | bytes 128
  942.5 18.4 %all-gather.20.cloned.1.call-done = bf16[6912,640]{0,1:T(8,128)(2,1)} async-done(((bf16[3456,640]{0,1:T(8,128)(2,1)}), bf16[6912,640]{0,1:T(8,128)(2,1)}) %all-gather.20.cloned.1.call-update) | async-done | bytes 8847376 | tf_op jit(solution)/shard_map/all_gather | solution.py:68
  967.2 21.6 %psum.107 = f32[128,1]{0,1:T(1,128)S(1)} all-reduce(f32[128,1]{0,1:T(1,128)S(1)} %bitcast.143), channel_id=1, replica_groups=mesh['groups'=2,'fsdp'=8,'dp'=2] {'fsdp'}, use_global_device_ids=true, to_apply=%region_35.0 | all-reduce | flops 128 | bytes 1024 | tf_op jit(solution)/shard_map/psum | solution.py:13
  989.7 39.9 %all-gather.22.cloned.1.call-done = bf16[128,5120]{1,0:T(8,128)(2,1)} async-done(((bf16[128,640]{1,0:T(8,128)(2,1)}), bf16[128,5120]{1,0:T(8,128)(2,1)}) %all-gather.22.cloned.1.call-update) | async-done | bytes 1310736 | tf_op jit(solution)/shard_map/all_gather | solution.py:29
  1041.1 19.1 %psum.108 = f32[128]{0:T(128)S(1)} all-reduce(f32[128]{0:T(128)S(1)} %get-tuple-element.29), channel_id=1, replica_groups=mesh['groups'=2,'fsdp'=8,'dp'=2] {'fsdp'}, use_global_device_ids=true, to_apply=%region_37.0 | all-reduce | flops 128 | bytes 1024 | tf_op jit(solution)/shard_map/psum | solution.py:13
  1073.6 62.5 %reduce-scatter.37.cloned.1.call-done = bf16[640,128]{1,0:T(8,128)(2,1)} async-done(((bf16[5120,128]{1,0:T(8,128)(2,1)}), bf16[640,128]{1,0:T(8,128)(2,1)}) %reduce-scatter.37.cloned.1.call-update) | async-done | bytes 163856
  1137.3 19.1 %psum.109 = f32[128,1]{0,1:T(1,128)S(1)} all-reduce(f32[128,1]{0,1:T(1,128)S(1)} %bitcast.140), channel_id=1, replica_groups=mesh['groups'=2,'fsdp'=8,'dp'=2] {'fsdp'}, use_global_device_ids=true, to_apply=%region_40.0 | all-reduce | flops 128 | bytes 1024 | tf_op jit(solution)/shard_map/psum | solution.py:13
  1205.3 33.8 %all-reduce.5 = f32[16]{0:T(128)S(1)} all-reduce(f32[16]{0:T(128)S(1)} %dynamic-update-slice.5), channel_id=1, replica_groups=mesh['groups'=2,'fsdp'=8,'dp'=2] {'fsdp','dp'}, use_global_device_ids=true, to_apply=%add.5 | all-reduce | flops 16 | bytes 128
  1250.9 18.1 %all-gather.24.cloned.1.call-done = bf16[6912,640]{0,1:T(8,128)(2,1)} async-done(((bf16[3456,640]{0,1:T(8,128)(2,1)}), bf16[6912,640]{0,1:T(8,128)(2,1)}) %all-gather.24.cloned.1.call-update) | async-done | bytes 8847376 | tf_op jit(solution)/shard_map/all_gather | solution.py:68
  1275.4 21.6 %psum.110 = f32[128,1]{0,1:T(1,128)S(1)} all-reduce(f32[128,1]{0,1:T(1,128)S(1)} %bitcast.144), channel_id=1, replica_groups=mesh['groups'=2,'fsdp'=8,'dp'=2] {'fsdp'}, use_global_device_ids=true, to_apply=%region_45.0 | all-reduce | flops 128 | bytes 1024 | tf_op jit(solution)/shard_map/psum | solution.py:13
  1297.9 39.9 %all-gather.26.cloned.1.call-done = bf16[128,5120]{1,0:T(8,128)(2,1)} async-done(((bf16[128,640]{1,0:T(8,128)(2,1)}), bf16[128,5120]{1,0:T(8,128)(2,1)}) %all-gather.26.cloned.1.call-update) | async-done | bytes 1310736 | tf_op jit(solution)/shard_map/all_gather | solution.py:29
  1348.6 19.5 %psum.111 = f32[128]{0:T(128)} all-reduce(f32[128]{0:T(128)S(1)} %fusion.21), channel_id=1, replica_groups=mesh['groups'=2,'fsdp'=8,'dp'=2] {'fsdp'}, use_global_device_ids=true, to_apply=%region_47.0 | all-reduce | flops 128 | bytes 1024 | tf_op jit(solution)/shard_map/psum | solution.py:13
  (139 shorter events, 386.2 us)
Async XLA Ops:
  6.5 1.5 copy-start
  6.5 70.6 %all-gather.10.cloned.1.call-start = ((), (), s32[]{:S(2)}) async-start(), calls=%async_computation.8 | async-start | bytes 1474560 | tf_op jit(solution)/shard_map/all_gather | solution.py:29
  37.1 145.8 %reduce-scatter.25.cloned.1.call-start = ((), (), s32[]{:S(2)}) async-start(), calls=%async_computation.17 | async-start | bytes 1474560
  37.2 70.2 %copy-start.5 = (s32[2048]{0:T(1024)}, s32[2048]{0:T(1024)S(1)}, u32[]{:S(2)}) copy-start(s32[2048]{0:T(1024)S(1)} %iota_add_fusion) | copy-start | bytes 24580
  37.2 70.2 %copy-start.7 = (s32[128]{0:T(128)S(1)}, s32[128]{0:T(128)}, u32[]{:S(2)}) copy-start(s32[128]{0:T(128)} %param.13) | copy-start | bytes 1540
  120.4 115.5 %reduce-scatter.27.cloned.1.call-start = ((), (), s32[]{:S(2)}) async-start(), calls=%async_computation.18 | async-start | bytes 13271040
  221.8 43.8 %all-gather.12.cloned.1.call-start = ((), (), s32[]{:S(2)}) async-start(), calls=%async_computation.9 | async-start | bytes 13271040 | tf_op jit(solution)/shard_map/all_gather | solution.py:68
  243.1 91.3 %copy-start.1 = (f32[128,2048]{1,0:T(8,128)S(1)}, f32[128,2048]{1,0:T(8,128)}, u32[]{:S(2)}) copy-start(f32[128,2048]{1,0:T(8,128)} %get-tuple-element.18) | copy-start | bytes 3145732
  243.1 91.2 %all-gather.14.cloned.1.call-start = ((), (), s32[]{:S(2)}) async-start(), calls=%async_computation.10 | async-start | bytes 1474560 | tf_op jit(solution)/shard_map/all_gather | solution.py:29
  294.4 146.3 %reduce-scatter.29.cloned.1.call-start = ((), (), s32[]{:S(2)}) async-start(), calls=%async_computation.19 | async-start | bytes 1474560
  378.2 115.5 %reduce-scatter.31.cloned.1.call-start = ((), (), s32[]{:S(2)}) async-start(), calls=%async_computation.20 | async-start | bytes 13271040
  479.8 0.7 copy-start.9
  479.8 131.8 %all-gather.16.cloned.1.call-start = ((), (), s32[]{:S(2)}) async-start(), calls=%async_computation.11 | async-start | bytes 13271040 | tf_op jit(solution)/shard_map/all_gather | solution.py:68
  593.2 87.2 %copy-start.2 = (f32[128,2048]{1,0:T(8,128)S(1)}, f32[128,2048]{1,0:T(8,128)}, u32[]{:S(2)}) copy-start(f32[128,2048]{1,0:T(8,128)} %get-tuple-element.18) | copy-start | bytes 3145732
  593.2 87.2 %all-gather.18.cloned.1.call-start = ((), (), s32[]{:S(2)}) async-start(), calls=%async_computation.12 | async-start | bytes 1474560 | tf_op jit(solution)/shard_map/all_gather | solution.py:29
  640.4 146.3 %reduce-scatter.33.cloned.1.call-start = ((), (), s32[]{:S(2)}) async-start(), calls=%async_computation.21 | async-start | bytes 1474560
  724.2 115.5 %reduce-scatter.35.cloned.1.call-start = ((), (), s32[]{:S(2)}) async-start(), calls=%async_computation.22 | async-start | bytes 13271040
  825.6 135.2 %all-gather.20.cloned.1.call-start = ((), (), s32[]{:S(2)}) async-start(), calls=%async_computation.13 | async-start | bytes 13271040 | tf_op jit(solution)/shard_map/all_gather | solution.py:68
  942.4 87.2 %copy-start.3 = (f32[128,2048]{1,0:T(8,128)S(1)}, f32[128,2048]{1,0:T(8,128)}, u32[]{:S(2)}) copy-start(f32[128,2048]{1,0:T(8,128)} %get-tuple-element.18) | copy-start | bytes 3145732
  942.4 87.2 %all-gather.22.cloned.1.call-start = ((), (), s32[]{:S(2)}) async-start(), calls=%async_computation.14 | async-start | bytes 1474560 | tf_op jit(solution)/shard_map/all_gather | solution.py:29
  989.7 146.4 %reduce-scatter.37.cloned.1.call-start = ((), (), s32[]{:S(2)}) async-start(), calls=%async_computation.23 | async-start | bytes 1474560
  1073.5 115.5 %reduce-scatter.39.cloned.1.call-start = ((), (), s32[]{:S(2)}) async-start(), calls=%async_computation.24 | async-start | bytes 13271040
  1175.0 94.1 %all-gather.24.cloned.1.call-start = ((), (), s32[]{:S(2)}) async-start(), calls=%async_computation.15 | async-start | bytes 13271040 | tf_op jit(solution)/shard_map/all_gather | solution.py:68
  1250.6 87.2 %copy-start.4 = (f32[128,2048]{1,0:T(8,128)S(1)}, f32[128,2048]{1,0:T(8,128)}, u32[]{:S(2)}) copy-start(f32[128,2048]{1,0:T(8,128)} %get-tuple-element.18) | copy-start | bytes 3145732
  1250.6 87.2 %copy-start.6 = (s32[2048]{0:T(1024)S(1)}, s32[2048]{0:T(1024)}, u32[]{:S(2)}) copy-start(s32[2048]{0:T(1024)} %copy-done.5) | copy-start | bytes 24580
  1250.6 87.2 %copy-start.8 = (s32[128]{0:T(128)S(1)}, s32[128]{0:T(128)}, u32[]{:S(2)}) copy-start(s32[128]{0:T(128)} %param.12) | copy-start | bytes 1540
  1250.7 87.2 %all-gather.26.cloned.1.call-start = ((), (), s32[]{:S(2)}) async-start(), calls=%async_computation.16 | async-start | bytes 1474560 | tf_op jit(solution)/shard_map/all_gather | solution.py:29
Sparse Core Ops, SparseCore 0:
  37.2 39.8 all-gather.9
  120.5 62.3 reduce-scatter.24
  221.9 13.9 reduce-scatter.26
  243.2 22.2 all-gather.11
  294.5 39.7 all-gather.13
  378.4 62.3 reduce-scatter.28
  479.9 13.8 reduce-scatter.30
  593.3 18.2 all-gather.15
  640.5 39.7 all-gather.17
  724.3 62.2 reduce-scatter.32
  825.7 13.9 reduce-scatter.34
  942.6 18.2 all-gather.19
  989.8 39.7 all-gather.21
  1073.7 62.3 reduce-scatter.36
  1175.1 13.9 reduce-scatter.38
  1250.8 18.2 all-gather.23
  1298.0 39.7 all-gather.25
